TPU v7x, 512 devices: a whole 4x8x8 slice. The times are simulated.
512 devices in a mesh: dp: 16 (over x_lo, y), tensor: 32 (over x_hi, z, core).
Axes of the slice: x: 4 (x_hi: 2, x_lo: 2; x = x_hi * 2 + x_lo), y: 8, z: 8, core: 2. Of those that a mesh axis runs over, the one named last changes fastest.
Arguments:
- tokens: bfloat16 [4096, 14336], P('dp', 'tensor'), may hold values from -6 to 6
- base_weight: bfloat16 [14336, 4096], P('tensor'), may hold values from -0.5 to 0.5
- adapter_down: bfloat16 [16, 14336, 16], P(None, 'tensor'), may hold values from -0.046875 to 0.046875
- adapter_up: bfloat16 [16, 16, 4096], P(None, None, 'tensor'), may hold values from -1.5 to 1.5
- magnitude: bfloat16 [16, 4096], P(None, 'tensor'), may hold values from 0.5 to 2
- seg_lengths: int32 [16], replicated, may hold values from 1 to 2048, 4096 in all
- cotangent: bfloat16 [4096, 4096], P('dp', 'tensor'), may hold values from -6 to 6
Outputs:
- projected: bfloat16 [4096, 4096], P('dp', 'tensor')
- grad_tokens: bfloat16 [4096, 14336], P('dp', 'tensor')
- grad_down: bfloat16 [16, 14336, 16], P(None, 'tensor')
- grad_up: float32 [16, 16, 4096], P(None, None, 'tensor')
- grad_magnitude: float32 [16, 4096], P(None, 'tensor')
Inputs may be any that keep to these rules, and one draw needn't show every extreme that they name: The segments cover all 4096 tokens in order: seg_lengths sums to 4096.
All inputs are finite; a program needn't handle non-finite values.
Results may differ from a plain program's by a relative error of at most 0.019.
Values may be sent and summed in bfloat16 or wider, within the bound.
No kernel may reach another device: no remote copies, remote signals or barrier semaphores. Data moves between devices by JAX's collectives and lax.ppermute only.
A program may use at most 64 MiB of HBM per device.

v0:
```python
import jax
import jax.numpy as jnp
from jax import lax
from jax.sharding import PartitionSpec as P

HIGHEST_MODE = lax.Precision.HIGHEST
EPSILON = 1e-06


def from_everyone(shard, axis):
    size = lax.axis_size(axis)
    return lax.all_to_all(
        jnp.broadcast_to(shard[None], (size, *shard.shape)), axis, 0, 0, tiled=True
    )


def taken_together(shard, axis):
    return from_everyone(shard, axis).sum(axis=0)


def split_up(shard, dim, size):
    lengths = shard.shape
    tiles = shard.reshape(*lengths[:dim], size, lengths[dim] // size, *lengths[dim + 1 :])
    return jnp.moveaxis(tiles, dim, 0)


def summed_on_arrival(shard, axis, dim):
    size = lax.axis_size(axis)
    tiles = lax.all_to_all(split_up(shard, dim, size), axis, 0, 0, tiled=True)
    return jnp.sum(tiles.astype(jnp.float32), axis=0)


def padded_to(lines, size):
    spare = -lines.shape[0] % size
    if not spare:
        return lines
    return jnp.concatenate([lines, jnp.zeros((spare, *lines.shape[1:]), lines.dtype)])


def laid_out(tiles, dim):
    lengths = list(tiles.shape[1:])
    lengths[dim] *= tiles.shape[0]
    return jnp.moveaxis(tiles, 0, dim).reshape(lengths)


def collect(shard, axis, dim):
    return laid_out(from_everyone(shard, axis), dim)


def total_of(shard, axes):
    lines = shard.reshape(-1, shard.shape[-1])
    own = summed_on_arrival(padded_to(lines, lax.axis_size(axes)), axes, 0)
    whole = collect(own.astype(jnp.bfloat16), axes, 0)
    return whole[: len(lines)].reshape(shard.shape).astype(jnp.float32)


def member_table(seg_lengths, first_token, token_count):
    seg_ends = jnp.cumsum(seg_lengths)
    seg_starts = seg_ends - seg_lengths
    positions = first_token + jnp.arange(token_count, dtype=jnp.int32)[:, None]
    return ((positions >= seg_starts[None, :]) & (positions < seg_ends[None, :])).astype(
        jnp.float32
    )


def pick_rank(member, spread):
    token_count, adapter_count = member.shape
    return jnp.einsum(
        "ta,tar->tr", member, spread.reshape(token_count, adapter_count, -1), precision=HIGHEST_MODE
    )


def expand_rank(member, low_rounded):
    widened = member[:, :, None] * low_rounded.astype(jnp.float32)[:, None, :]
    return widened.reshape(member.shape[0], -1).astype(jnp.bfloat16)


def local(tokens, base_weight, adapter_down, adapter_up, magnitude, seg_lengths, cotangent):
    token_count, own_rows = tokens.shape
    adapter_count, _, rank_width = adapter_down.shape
    own_width = adapter_up.shape[2]
    full_width = base_weight.shape[1]
    member = member_table(seg_lengths, lax.axis_index("dp") * token_count, token_count)
    down_flat = jnp.transpose(adapter_down, (1, 0, 2)).reshape(own_rows, adapter_count * rank_width)
    up_whole = lax.all_gather(adapter_up, "tensor", axis=2, tiled=True)
    spread = jnp.dot(tokens, down_flat, preferred_element_type=jnp.float32)
    low_rank = taken_together(pick_rank(member, spread), "tensor")
    low_wide = expand_rank(member, low_rank.astype(jnp.bfloat16))
    cross_terms = lax.dot_general(
        down_flat, base_weight, (((0,), (0,)), ((), ())), preferred_element_type=jnp.float32
    )
    up_float = up_whole.astype(jnp.float32)
    gram_matrix = jnp.einsum(
        "afr,afs->ars", adapter_down, adapter_down, preferred_element_type=jnp.float32
    )
    column_squares = jnp.sum(jnp.square(base_weight.astype(jnp.float32)), axis=0)
    cross_sum = jnp.sum(
        cross_terms.reshape(adapter_count, rank_width, full_width) * up_float, axis=1
    )
    gram_sum = jnp.sum(
        up_float * jnp.einsum("ars,asd->ard", gram_matrix, up_float, precision=HIGHEST_MODE), axis=1
    )
    partial_squares = column_squares[None, :] + 2.0 * cross_sum + gram_sum
    base_terms = jnp.dot(tokens, base_weight, preferred_element_type=jnp.float32)
    col_norms = jnp.sqrt(
        summed_on_arrival(partial_squares.astype(jnp.bfloat16), "tensor", 1) + EPSILON
    )
    base_own = summed_on_arrival(base_terms.astype(jnp.bfloat16), "tensor", 1)
    up_own = adapter_up.reshape(adapter_count * rank_width, own_width)
    hidden = base_own + jnp.dot(low_wide, up_own, preferred_element_type=jnp.float32)
    col_scale = magnitude.astype(jnp.float32) / col_norms
    token_scale = jnp.dot(member, col_scale, precision=HIGHEST_MODE)
    projected = (hidden * token_scale).astype(jnp.bfloat16)
    grad_in = cotangent.astype(jnp.float32)
    grad_mag_part = jnp.dot(member.T, grad_in * hidden, precision=HIGHEST_MODE)
    grad_own = (grad_in * token_scale).astype(jnp.bfloat16)
    grad_up_part = jnp.dot(low_wide.T, grad_own, preferred_element_type=jnp.float32)
    grad_up_part = grad_up_part.reshape(adapter_count, rank_width, own_width)
    back_spread = lax.dot_general(
        grad_own, up_own, (((1,), (1,)), ((), ())), preferred_element_type=jnp.float32
    )
    back_rank = taken_together(pick_rank(member, back_spread), "tensor")
    back_wide = expand_rank(member, back_rank.astype(jnp.bfloat16))
    start_grad = lax.dot_general(
        back_wide, down_flat, (((1,), (1,)), ((), ())), preferred_element_type=jnp.float32
    )
    grad_base = start_grad + lax.dot_general(
        lax.all_gather(grad_own, "tensor", axis=1, tiled=True),
        base_weight,
        (((1,), (1,)), ((), ())),
        preferred_element_type=jnp.float32,
    )
    grad_tokens = grad_base.astype(jnp.bfloat16)
    grad_down_part = lax.dot_general(
        tokens, back_wide, (((0,), (0,)), ((), ())), preferred_element_type=jnp.float32
    )
    grad_down_part = jnp.transpose(
        grad_down_part.reshape(own_rows, adapter_count, rank_width), (1, 0, 2)
    )
    mag_summed, up_summed, down_summed = (
        total_of(grad_mag_part.astype(jnp.bfloat16), "dp"),
        total_of(grad_up_part.astype(jnp.bfloat16), "dp"),
        total_of(grad_down_part.astype(jnp.bfloat16), "dp"),
    )
    grad_magnitude = mag_summed / col_norms
    return (projected, grad_tokens, down_summed.astype(jnp.bfloat16), up_summed, grad_magnitude)


def solution(mesh):
    placed = (
        P("dp", "tensor"),
        P("tensor", None),
        P(None, "tensor", None),
        P(None, None, "tensor"),
        P(None, "tensor"),
        P(),
        P("dp", "tensor"),
    )
    return jax.shard_map(
        local,
        mesh=mesh,
        in_specs=placed,
        out_specs=(
            P("dp", "tensor"),
            P("dp", "tensor"),
            P(None, "tensor", None),
            P(None, None, "tensor"),
            P(None, "tensor"),
        ),
        check_vma=False,
    )
```

profile of v0, /device:TPU:8, one launch (start us, length us, event | category | flops | bytes accessed | tf_op | source)
XLA Modules:
  0.0 259.1 jit_solution(895637971586263253)
XLA Ops:
  9.6 1.2 fusion.9
  11.6 13.2 %all-to-all-start.1 = ((f32[32,256,16]{1,2,0:T(8,128)}), f32[32,256,16]{1,2,0:T(8,128)S(1)}, u32[]{:S(2)}, u32[]{:S(2)}) async-start(f32[32,256,16]{1,2,0:T(8,128)} %broadcast_in_dim.10), calls=%async_computation.1 | async-start | bytes 1048576 | tf_op jit(solution)/shard_map/all_to_all | solution.py:12
  24.8 3.5 %fusion.5 = bf16[32,32,8,128]{3,2,1,0:T(8,128)(2,1)S(1)} fusion(bf16[256,448]{0,1:T(8,128)(2,1)} %param.7, bf16[448,4096]{1,0:T(8,128)(2,1)} %param.8), kind=kOutput, calls=%fused_computation.9 | convolution fusion | flops 940572672 | bytes 5996544 | tf_op jit(solution)/shard_map/dot_general | solution.py:104
  28.2 1.9 copy.37
  30.1 15.0 %all-to-all-done.1 = f32[32,256,16]{1,2,0:T(8,128)S(1)} async-done(((f32[32,256,16]{1,2,0:T(8,128)}), f32[32,256,16]{1,2,0:T(8,128)S(1)}, u32[]{:S(2)}, u32[]{:S(2)}) %all-to-all-start.1) | async-done | bytes 524320 | tf_op jit(solution)/shard_map/all_to_all | solution.py:12
  45.1 4.0 %all-to-all-start = ((bf16[32,256,128]{2,1,0:T(8,128)(2,1)}), bf16[32,256,128]{2,1,0:T(8,128)(2,1)S(1)}, u32[]{:S(2)}, u32[]{:S(2)}) async-start(bf16[32,256,128]{2,1,0:T(8,128)(2,1)} %bitcast.86), calls=%async_computation | async-start | bytes 4194304 | tf_op jit(solution)/shard_map/all_to_all | solution.py:29
  49.4 2.8 %multiply_reduce_fusion = f32[4096]{0:T(1024)S(1)} fusion(bf16[448,4096]{1,0:T(8,128)(2,1)} %param.8), kind=kLoop, calls=%fused_computation | loop fusion | flops 5500928 | bytes 3686400 | tf_op jit(solution)/shard_map/reduce_sum | solution.py:96
  52.2 59.5 %all-gather.3.cloned.1.call-done = bf16[16,16,4096]{2,1,0:T(8,128)(2,1)} async-done(((bf16[16,16,128]{2,1,0:T(8,128)(2,1)}), bf16[16,16,4096]{2,1,0:T(8,128)(2,1)}) %all-gather.3.cloned.1.call-update) | async-done | bytes 2097168 | tf_op jit(solution)/shard_map/all_gather | solution.py:85
  111.8 4.7 %fusion.4 = f32[16,4096]{1,0:T(8,128)S(1)} fusion(f32[16,16,16]{2,1,0:T(8,128)S(1)} %fusion.40, bf16[16,16,4096]{2,1,0:T(8,128)(2,1)} %all-gather.3.cloned.1.call-done), kind=kOutput, calls=%fused_computation.8 | convolution fusion | flops 204406784 | bytes 2375680 | tf_op jit(solution)/shard_map/ars,asd->ard/dot_general | solution.py:101
  116.6 4.3 %fusion.1 = f32[16,4096]{1,0:T(8,128)S(1)} fusion(bf16[16,16,4096]{2,1,0:T(8,128)(2,1)} %all-gather.3.cloned.1.call-done, bf16[448,4096]{1,0:T(8,128)(2,1)} %param.8, bf16[16,448,16]{1,2,0:T(8,128)(2,1)S(1)} %copy-done), kind=kOutput, calls=%fused_computation.7 | convolution fusion | flops 942604288 | bytes 6258688 | tf_op jit(solution)/shard_map/dot_general | solution.py:89
  121.8 6.6 %all-to-all-start.2 = ((bf16[32,16,128]{2,1,0:T(8,128)(2,1)}), bf16[32,16,128]{2,1,0:T(8,128)(2,1)S(1)}, u32[]{:S(2)}, u32[]{:S(2)}) async-start(bf16[32,16,128]{2,1,0:T(8,128)(2,1)} %copy.21), calls=%async_computation.2 | async-start | bytes 262144 | tf_op jit(solution)/shard_map/all_to_all | solution.py:29
  128.9 11.3 %all-to-all-done.2 = bf16[32,16,128]{2,1,0:T(8,128)(2,1)S(1)} async-done(((bf16[32,16,128]{2,1,0:T(8,128)(2,1)}), bf16[32,16,128]{2,1,0:T(8,128)(2,1)S(1)}, u32[]{:S(2)}, u32[]{:S(2)}) %all-to-all-start.2) | async-done | bytes 131104 | tf_op jit(solution)/shard_map/all_to_all | solution.py:29
  140.3 1.0 fusion.19
  142.2 7.8 %all-to-all-start.8 = ((bf16[16,1,128]{2,1,0:T(2,128)(2,1)}), bf16[16,1,128]{2,1,0:T(2,128)(2,1)S(1)}, u32[]{:S(2)}, u32[]{:S(2)}) async-start(bf16[16,1,128]{2,1,0:T(2,128)(2,1)} %copy.23), calls=%async_computation.8 | async-start | bytes 16384 | tf_op jit(solution)/shard_map/all_to_all | solution.py:29
  150.0 1.0 fusion.10
  151.1 6.0 %all-to-all-done.8 = bf16[16,1,128]{2,1,0:T(2,128)(2,1)S(1)} async-done(((bf16[16,1,128]{2,1,0:T(2,128)(2,1)}), bf16[16,1,128]{2,1,0:T(2,128)(2,1)S(1)}, u32[]{:S(2)}, u32[]{:S(2)}) %all-to-all-start.8) | async-done | bytes 4128 | tf_op jit(solution)/shard_map/all_to_all | solution.py:29
  157.1 0.9 broadcast_in_dim.11
  157.9 3.9 %all-to-all-start.3 = ((f32[32,256,16]{1,2,0:T(8,128)}), f32[32,256,16]{1,2,0:T(8,128)S(1)}, u32[]{:S(2)}, u32[]{:S(2)}) async-start(f32[32,256,16]{1,2,0:T(8,128)} %broadcast_in_dim.11), calls=%async_computation.3 | async-start | bytes 1048576 | tf_op jit(solution)/shard_map/all_to_all | solution.py:12
  161.9 1.6 convolution_convert_fusion.2
  163.5 18.5 %all-to-all-done.3 = f32[32,256,16]{1,2,0:T(8,128)S(1)} async-done(((f32[32,256,16]{1,2,0:T(8,128)}), f32[32,256,16]{1,2,0:T(8,128)S(1)}, u32[]{:S(2)}, u32[]{:S(2)}) %all-to-all-start.3) | async-done | bytes 524320 | tf_op jit(solution)/shard_map/all_to_all | solution.py:12
  182.6 4.5 %all-to-all-start.9 = ((bf16[16,1,128]{2,1,0:T(2,128)(2,1)}), bf16[16,1,128]{2,1,0:T(2,128)(2,1)S(1)}, u32[]{:S(2)}, u32[]{:S(2)}) async-start(bf16[16,1,128]{2,1,0:T(2,128)(2,1)} %broadcast_in_dim.14), calls=%async_computation.9 | async-start | bytes 16384 | tf_op jit(solution)/shard_map/all_to_all | solution.py:12
  187.2 7.1 %all-to-all-done.9 = bf16[16,1,128]{2,1,0:T(2,128)(2,1)S(1)} async-done(((bf16[16,1,128]{2,1,0:T(2,128)(2,1)}), bf16[16,1,128]{2,1,0:T(2,128)(2,1)S(1)}, u32[]{:S(2)}, u32[]{:S(2)}) %all-to-all-start.9) | async-done | bytes 4128 | tf_op jit(solution)/shard_map/all_to_all | solution.py:12
  194.2 4.7 %all-to-all-start.6 = ((bf16[16,16,128]{2,1,0:T(8,128)(2,1)}), bf16[16,16,128]{2,1,0:T(8,128)(2,1)S(1)}, u32[]{:S(2)}, u32[]{:S(2)}) async-start(bf16[16,16,128]{2,1,0:T(8,128)(2,1)} %convolution_convert_fusion.2), calls=%async_computation.6 | async-start | bytes 131072 | tf_op jit(solution)/shard_map/all_to_all | solution.py:29
  200.1 6.5 %all-to-all-done.6 = bf16[16,16,128]{2,1,0:T(8,128)(2,1)S(1)} async-done(((bf16[16,16,128]{2,1,0:T(8,128)(2,1)}), bf16[16,16,128]{2,1,0:T(8,128)(2,1)S(1)}, u32[]{:S(2)}, u32[]{:S(2)}) %all-to-all-start.6) | async-done | bytes 65568 | tf_op jit(solution)/shard_map/all_to_all | solution.py:29
  206.6 4.4 %all-to-all-start.4 = ((bf16[16,448,16]{1,2,0:T(8,128)(2,1)}), bf16[16,448,16]{1,2,0:T(8,128)(2,1)S(1)}, u32[]{:S(2)}, u32[]{:S(2)}) async-start(bf16[16,448,16]{1,2,0:T(8,128)(2,1)} %bitcast.19), calls=%async_computation.4 | async-start | bytes 524288 | tf_op jit(solution)/shard_map/all_to_all | solution.py:29
  211.0 9.1 %all-to-all-done.4 = bf16[16,448,16]{1,2,0:T(8,128)(2,1)S(1)} async-done(((bf16[16,448,16]{1,2,0:T(8,128)(2,1)}), bf16[16,448,16]{1,2,0:T(8,128)(2,1)S(1)}, u32[]{:S(2)}, u32[]{:S(2)}) %all-to-all-start.4) | async-done | bytes 229408 | tf_op jit(solution)/shard_map/all_to_all | solution.py:29
  220.7 4.2 %all-to-all-start.7 = ((bf16[16,16,128]{2,1,0:T(8,128)(2,1)}), bf16[16,16,128]{2,1,0:T(8,128)(2,1)S(1)}, u32[]{:S(2)}, u32[]{:S(2)}) async-start(bf16[16,16,128]{2,1,0:T(8,128)(2,1)} %broadcast_in_dim.13), calls=%async_computation.7 | async-start | bytes 131072 | tf_op jit(solution)/shard_map/all_to_all | solution.py:12
  225.0 7.6 %all-to-all-done.7 = bf16[16,16,128]{2,1,0:T(8,128)(2,1)S(1)} async-done(((bf16[16,16,128]{2,1,0:T(8,128)(2,1)}), bf16[16,16,128]{2,1,0:T(8,128)(2,1)S(1)}, u32[]{:S(2)}, u32[]{:S(2)}) %all-to-all-start.7) | async-done | bytes 65568 | tf_op jit(solution)/shard_map/all_to_all | solution.py:12
  233.3 4.3 %all-to-all-start.5 = ((bf16[16,448,16]{1,2,0:T(8,128)(2,1)}), bf16[16,448,16]{1,2,0:T(8,128)(2,1)S(1)}, u32[]{:S(2)}, u32[]{:S(2)}) async-start(bf16[16,448,16]{1,2,0:T(8,128)(2,1)} %broadcast_in_dim.12), calls=%async_computation.5 | async-start | bytes 524288 | tf_op jit(solution)/shard_map/all_to_all | solution.py:12
  238.9 7.8 %all-to-all-done.5 = bf16[16,448,16]{1,2,0:T(8,128)(2,1)S(1)} async-done(((bf16[16,448,16]{1,2,0:T(8,128)(2,1)}), bf16[16,448,16]{1,2,0:T(8,128)(2,1)S(1)}, u32[]{:S(2)}, u32[]{:S(2)}) %all-to-all-start.5) | async-done | bytes 229408 | tf_op jit(solution)/shard_map/all_to_all | solution.py:12
  246.7 3.8 %fusion.41 = f32[256,448]{0,1:T(8,128)S(1)} fusion(bf16[256,4096]{1,0:T(8,128)(2,1)} %all-gather.5.cloned.1.call-done, bf16[448,4096]{1,0:T(8,128)(2,1)} %param.8), kind=kOutput, calls=%fused_computation.65 | convolution fusion | flops 939524096 | bytes 6225920 | tf_op jit(solution)/shard_map/dot_general | solution.py:127
  250.5 1.0 fusion.7
  (51 shorter events, 11.0 us)
Async XLA Ops:
  7.2 2.4 copy-start
  7.2 104.6 %all-gather.3.cloned.1.call-start = ((), (), s32[]{:S(2)}) async-start(), calls=%async_computation.10 | async-start | bytes 2162688 | tf_op jit(solution)/shard_map/all_gather | solution.py:85
  11.6 33.5 %all-to-all-start.1 = ((f32[32,256,16]{1,2,0:T(8,128)}), f32[32,256,16]{1,2,0:T(8,128)S(1)}, u32[]{:S(2)}, u32[]{:S(2)}) async-start(f32[32,256,16]{1,2,0:T(8,128)} %broadcast_in_dim.10), calls=%async_computation.1 | async-start | bytes 1048576 | tf_op jit(solution)/shard_map/all_to_all | solution.py:12
  45.1 76.6 %all-to-all-start = ((bf16[32,256,128]{2,1,0:T(8,128)(2,1)}), bf16[32,256,128]{2,1,0:T(8,128)(2,1)S(1)}, u32[]{:S(2)}, u32[]{:S(2)}) async-start(bf16[32,256,128]{2,1,0:T(8,128)(2,1)} %bitcast.86), calls=%async_computation | async-start | bytes 4194304 | tf_op jit(solution)/shard_map/all_to_all | solution.py:29
  120.9 7.8 %copy-start.3 = (bf16[16,16,128]{2,1,0:T(8,128)(2,1)S(1)}, bf16[16,16,128]{2,1,0:T(8,128)(2,1)}, u32[]{:S(2)}) copy-start(bf16[16,16,128]{2,1,0:T(8,128)(2,1)} %param.10) | copy-start | bytes 196612
  120.9 19.4 %copy-start.2 = (bf16[256,128]{1,0:T(8,128)(2,1)S(1)}, bf16[256,128]{1,0:T(8,128)(2,1)}, u32[]{:S(2)}) copy-start(bf16[256,128]{1,0:T(8,128)(2,1)} %param.13) | copy-start | bytes 196612
  120.9 19.4 %copy-start.4 = (bf16[16,128]{1,0:T(8,128)(2,1)S(1)}, bf16[16,128]{1,0:T(8,128)(2,1)}, u32[]{:S(2)}) copy-start(bf16[16,128]{1,0:T(8,128)(2,1)} %param.11) | copy-start | bytes 12292
  121.1 77.9 %copy-start.1 = (bf16[256,448]{0,1:T(8,128)(2,1)S(1)}, bf16[256,448]{0,1:T(8,128)(2,1)}, u32[]{:S(2)}) copy-start(bf16[256,448]{0,1:T(8,128)(2,1)} %param.7) | copy-start | bytes 688132
  121.8 18.5 %all-to-all-start.2 = ((bf16[32,16,128]{2,1,0:T(8,128)(2,1)}), bf16[32,16,128]{2,1,0:T(8,128)(2,1)S(1)}, u32[]{:S(2)}, u32[]{:S(2)}) async-start(bf16[32,16,128]{2,1,0:T(8,128)(2,1)} %copy.21), calls=%async_computation.2 | async-start | bytes 262144 | tf_op jit(solution)/shard_map/all_to_all | solution.py:29
  128.3 118.4 %all-gather.5.cloned.1.call-start = ((), (), s32[]{:S(2)}) async-start(), calls=%async_computation.11 | async-start | bytes 2162688 | tf_op jit(solution)/shard_map/all_gather | solution.py:128
  142.2 14.9 %all-to-all-start.8 = ((bf16[16,1,128]{2,1,0:T(2,128)(2,1)}), bf16[16,1,128]{2,1,0:T(2,128)(2,1)S(1)}, u32[]{:S(2)}, u32[]{:S(2)}) async-start(bf16[16,1,128]{2,1,0:T(2,128)(2,1)} %copy.23), calls=%async_computation.8 | async-start | bytes 16384 | tf_op jit(solution)/shard_map/all_to_all | solution.py:29
  157.9 24.1 %all-to-all-start.3 = ((f32[32,256,16]{1,2,0:T(8,128)}), f32[32,256,16]{1,2,0:T(8,128)S(1)}, u32[]{:S(2)}, u32[]{:S(2)}) async-start(f32[32,256,16]{1,2,0:T(8,128)} %broadcast_in_dim.11), calls=%async_computation.3 | async-start | bytes 1048576 | tf_op jit(solution)/shard_map/all_to_all | solution.py:12
  182.6 11.6 %all-to-all-start.9 = ((bf16[16,1,128]{2,1,0:T(2,128)(2,1)}), bf16[16,1,128]{2,1,0:T(2,128)(2,1)S(1)}, u32[]{:S(2)}, u32[]{:S(2)}) async-start(bf16[16,1,128]{2,1,0:T(2,128)(2,1)} %broadcast_in_dim.14), calls=%async_computation.9 | async-start | bytes 16384 | tf_op jit(solution)/shard_map/all_to_all | solution.py:12
  194.2 12.4 %all-to-all-start.6 = ((bf16[16,16,128]{2,1,0:T(8,128)(2,1)}), bf16[16,16,128]{2,1,0:T(8,128)(2,1)S(1)}, u32[]{:S(2)}, u32[]{:S(2)}) async-start(bf16[16,16,128]{2,1,0:T(8,128)(2,1)} %convolution_convert_fusion.2), calls=%async_computation.6 | async-start | bytes 131072 | tf_op jit(solution)/shard_map/all_to_all | solution.py:29
  206.6 13.5 %all-to-all-start.4 = ((bf16[16,448,16]{1,2,0:T(8,128)(2,1)}), bf16[16,448,16]{1,2,0:T(8,128)(2,1)S(1)}, u32[]{:S(2)}, u32[]{:S(2)}) async-start(bf16[16,448,16]{1,2,0:T(8,128)(2,1)} %bitcast.19), calls=%async_computation.4 | async-start | bytes 524288 | tf_op jit(solution)/shard_map/all_to_all | solution.py:29
  220.7 11.8 %all-to-all-start.7 = ((bf16[16,16,128]{2,1,0:T(8,128)(2,1)}), bf16[16,16,128]{2,1,0:T(8,128)(2,1)S(1)}, u32[]{:S(2)}, u32[]{:S(2)}) async-start(bf16[16,16,128]{2,1,0:T(8,128)(2,1)} %broadcast_in_dim.13), calls=%async_computation.7 | async-start | bytes 131072 | tf_op jit(solution)/shard_map/all_to_all | solution.py:12
  233.3 13.5 %all-to-all-start.5 = ((bf16[16,448,16]{1,2,0:T(8,128)(2,1)}), bf16[16,448,16]{1,2,0:T(8,128)(2,1)S(1)}, u32[]{:S(2)}, u32[]{:S(2)}) async-start(bf16[16,448,16]{1,2,0:T(8,128)(2,1)} %broadcast_in_dim.12), calls=%async_computation.5 | async-start | bytes 524288 | tf_op jit(solution)/shard_map/all_to_all | solution.py:12
Sparse Core Ops, SparseCore 0:
  11.1 100.6 all-gather.2
  141.5 80.5 all-gather.4
where the time goes:
time: 260 us; the launch traced here: 259 us
  waiting for transfers between devices  149 us (57%)
  starting transfers between devices  57.6 us (22%)
  matrix products  23 us (9%)
  between operations  14.3 us (6%)
  local copies, waits for them, and re-layouts  9.3 us (4%)
  other arithmetic  5.62 us (2%)
    all_gather x1, waiting for transfers between devices, local(): up_whole = lax.all_gather(adapter_up, 'tensor', axis=2, tiled=True)  59.5 us
    all_to_all x5, waiting for transfers between devices, from_everyone(): lax.all_to_all(jnp.broadcast_to(shard[None], (size, *shard.shape)), axis,...  55.9 us
    all_to_all x5, waiting for transfers between devices, summed_on_arrival(): tiles = lax.all_to_all(split_up(shard, dim, size), axis, 0, 0, tiled=True)  33 us
    all_to_all x5, starting transfers between devices, from_everyone(): lax.all_to_all(jnp.broadcast_to(shard[None], (size, *shard.shape)), axis,...  30.1 us
    all_to_all x5, starting transfers between devices, summed_on_arrival(): tiles = lax.all_to_all(split_up(shard, dim, size), axis, 0, 0, tiled=True)  27.5 us
  transfers between devices with their start and end apart: 12, of which 10 were waited for; matrix products, arithmetic and copies ran while one was open for 12% of the time, Pallas kernels for 0%

commit v1 on v0

--- a/solution.py
+++ b/solution.py
@@ -82,7 +82,9 @@
     full_width = base_weight.shape[1]
     member = member_table(seg_lengths, lax.axis_index("dp") * token_count, token_count)
     down_flat = jnp.transpose(adapter_down, (1, 0, 2)).reshape(own_rows, adapter_count * rank_width)
-    up_whole = lax.all_gather(adapter_up, "tensor", axis=2, tiled=True)
+    up_whole = jnp.concatenate(
+        lax.all_to_all(jnp.stack([adapter_up] * lax.axis_size("tensor")), "tensor", 0, 0), axis=2
+    )
     spread = jnp.dot(tokens, down_flat, preferred_element_type=jnp.float32)
     low_rank = taken_together(pick_rank(member, spread), "tensor")
     low_wide = expand_rank(member, low_rank.astype(jnp.bfloat16))

time: 260 us -> 295 us (1.13)
  blocking collectives: 0 us -> 32.9 us
  waiting for transfers between devices: 149 us -> 162 us
  starting transfers between devices: 57.6 us -> 46.8 us
  matrix products: 23 us -> 20 us
    all_gather x1 -> x0, waiting for transfers between devices: 59.5 us -> none  [local(): up_whole = lax.all_gather(adapter_up, 'tensor', axis=2, tiled=True)]
    all_to_all x0 -> x1, waiting for transfers between devices: none -> 46.6 us  [local(): lax.all_to_all(jnp.stack([adapter_up] * lax.axis_size('tensor')), 'tensor...]
    all_to_all x5, waiting for transfers between devices: 33 us -> 73.8 us  [summed_on_arrival(): tiles = lax.all_to_all(split_up(shard, dim, size), axis, 0, 0, tiled=True)]
    all_to_all x0 -> x1, blocking collectives: none -> 32.9 us  [from_everyone(): lax.all_to_all(jnp.broadcast_to(shard[None], (size, *shard.shape)), axis,...]
    all_to_all x5 -> x4, waiting for transfers between devices: 55.9 us -> 41.8 us  [from_everyone(): lax.all_to_all(jnp.broadcast_to(shard[None], (size, *shard.shape)), axis,...]
    all_to_all x5 -> x4, starting transfers between devices: 30.1 us -> 16.9 us  [from_everyone(): lax.all_to_all(jnp.broadcast_to(shard[None], (size, *shard.shape)), axis,...]
    all_to_all x0 -> x1, starting transfers between devices: none -> 4.14 us  [local(): lax.all_to_all(jnp.stack([adapter_up] * lax.axis_size('tensor')), 'tensor...]
  transfers between devices with their start and end apart: 12 -> 11, of which waited for: 10 -> 10; matrix products, arithmetic and copies ran while one was open for 12% -> 8% of each run, Pallas kernels for 0% -> 0%
where the time goes in v1:
time: 295 us; the launch traced here: 294 us
  waiting for transfers between devices  162 us (55%)
  starting transfers between devices  46.8 us (16%)
  blocking collectives  32.9 us (11%)
  matrix products  20 us (7%)
  between operations  14.3 us (5%)
  local copies, waits for them, and re-layouts  11.7 us (4%)
  other arithmetic  5.62 us (2%)
    all_to_all x5, waiting for transfers between devices, summed_on_arrival(): tiles = lax.all_to_all(split_up(shard, dim, size), axis, 0, 0, tiled=True)  73.8 us
    all_to_all x1, waiting for transfers between devices, local(): lax.all_to_all(jnp.stack([adapter_up] * lax.axis_size('tensor')), 'tensor...  46.6 us
    all_to_all x4, waiting for transfers between devices, from_everyone(): lax.all_to_all(jnp.broadcast_to(shard[None], (size, *shard.shape)), axis,...  41.8 us
    all_to_all x1, blocking collectives, from_everyone(): lax.all_to_all(jnp.broadcast_to(shard[None], (size, *shard.shape)), axis,...  32.9 us
    all_to_all x5, starting transfers between devices, summed_on_arrival(): tiles = lax.all_to_all(split_up(shard, dim, size), axis, 0, 0, tiled=True)  25.8 us
    all_to_all x4, starting transfers between devices, from_everyone(): lax.all_to_all(jnp.broadcast_to(shard[None], (size, *shard.shape)), axis,...  16.9 us
  transfers between devices with their start and end apart: 11, of which 10 were waited for; matrix products, arithmetic and copies ran while one was open for 8% of the time, Pallas kernels for 0%

profile of v1, /device:TPU:8, one launch (start us, length us, event | category | flops | bytes accessed | tf_op | source)
XLA Modules:
  0.0 293.5 jit_solution(8180635275563733110)
XLA Ops:
  8.9 1.2 fusion.13
  10.1 32.9 %all_to_all.55 = f32[32,256,16]{1,2,0:T(8,128)S(1)} all-to-all(f32[32,256,16]{1,2,0:T(8,128)S(1)} %broadcast_in_dim.10), channel_id=1, replica_groups=mesh['dp'=16,'tensor'=32] {'tensor'}, dimensions={0} | all-to-all | bytes 1048576 | tf_op jit(solution)/shard_map/all_to_all | solution.py:12
  43.0 1.8 stack.2
  44.8 4.1 %all-to-all-start.2 = ((bf16[32,16,16,128]{3,2,1,0:T(8,128)(2,1)}), bf16[32,16,16,128]{3,2,1,0:T(8,128)(2,1)S(1)}, u32[]{:S(2)}, u32[]{:S(2)}) async-start(bf16[32,16,16,128]{3,2,1,0:T(8,128)(2,1)} %stack.2), calls=%async_computation.2 | async-start | bytes 4194304 | tf_op jit(solution)/shard_map/all_to_all | solution.py:86
  48.9 3.3 %fusion.9 = bf16[32,32,8,128]{3,2,1,0:T(8,128)(2,1)S(1)} fusion(bf16[256,448]{0,1:T(8,128)(2,1)S(1)} %copy-done.3, bf16[448,4096]{1,0:T(8,128)(2,1)} %param.8), kind=kOutput, calls=%fused_computation.11 | convolution fusion | flops 940572672 | bytes 5996544 | tf_op jit(solution)/shard_map/dot_general | solution.py:106
  52.3 1.9 copy.49
  54.2 46.6 %all-to-all-done.2 = bf16[32,16,16,128]{3,2,1,0:T(8,128)(2,1)S(1)} async-done(((bf16[32,16,16,128]{3,2,1,0:T(8,128)(2,1)}), bf16[32,16,16,128]{3,2,1,0:T(8,128)(2,1)S(1)}, u32[]{:S(2)}, u32[]{:S(2)}) %all-to-all-start.2) | async-done | bytes 2097184 | tf_op jit(solution)/shard_map/all_to_all | solution.py:86
  100.8 1.3 copy-done.1
  102.1 4.5 %all-to-all-start = ((bf16[32,256,128]{2,1,0:T(8,128)(2,1)}), bf16[32,256,128]{2,1,0:T(8,128)(2,1)S(1)}, u32[]{:S(2)}, u32[]{:S(2)}) async-start(bf16[32,256,128]{2,1,0:T(8,128)(2,1)} %bitcast.101), calls=%async_computation | async-start | bytes 4194304 | tf_op jit(solution)/shard_map/all_to_all | solution.py:29
  106.8 2.8 multiply_reduce_fusion
  109.7 4.4 %fusion.6 = f32[16,4096]{1,0:T(8,128)S(1)} fusion(bf16[448,4096]{1,0:T(8,128)(2,1)} %param.8, bf16[16,448,16]{1,2,0:T(8,128)(2,1)S(1)} %copy-done, bf16[32,16,16,128]{3,2,1,0:T(8,128)(2,1)} %copy-done.1), kind=kOutput, calls=%fused_computation.10 | convolution fusion | flops 942604288 | bytes 6258688 | tf_op jit(solution)/shard_map/dot_general | solution.py:91
  114.2 2.6 fusion.3
  117.7 40.8 %all-to-all-done = bf16[32,256,128]{2,1,0:T(8,128)(2,1)S(1)} async-done(((bf16[32,256,128]{2,1,0:T(8,128)(2,1)}), bf16[32,256,128]{2,1,0:T(8,128)(2,1)S(1)}, u32[]{:S(2)}, u32[]{:S(2)}) %all-to-all-start) | async-done | bytes 2097184 | tf_op jit(solution)/shard_map/all_to_all | solution.py:29
  158.5 4.5 %all-to-all-start.3 = ((bf16[32,16,128]{2,1,0:T(8,128)(2,1)}), bf16[32,16,128]{2,1,0:T(8,128)(2,1)S(1)}, u32[]{:S(2)}, u32[]{:S(2)}) async-start(bf16[32,16,128]{2,1,0:T(8,128)(2,1)} %copy.23), calls=%async_computation.3 | async-start | bytes 262144 | tf_op jit(solution)/shard_map/all_to_all | solution.py:29
  163.6 11.4 %all-to-all-done.3 = bf16[32,16,128]{2,1,0:T(8,128)(2,1)S(1)} async-done(((bf16[32,16,128]{2,1,0:T(8,128)(2,1)}), bf16[32,16,128]{2,1,0:T(8,128)(2,1)S(1)}, u32[]{:S(2)}, u32[]{:S(2)}) %all-to-all-start.3) | async-done | bytes 131104 | tf_op jit(solution)/shard_map/all_to_all | solution.py:29
  175.0 1.0 fusion.23
  176.9 7.6 %all-to-all-start.9 = ((bf16[16,1,128]{2,1,0:T(2,128)(2,1)}), bf16[16,1,128]{2,1,0:T(2,128)(2,1)S(1)}, u32[]{:S(2)}, u32[]{:S(2)}) async-start(bf16[16,1,128]{2,1,0:T(2,128)(2,1)} %copy.25), calls=%async_computation.9 | async-start | bytes 16384 | tf_op jit(solution)/shard_map/all_to_all | solution.py:29
  184.5 1.0 fusion.14
  185.5 6.0 %all-to-all-done.9 = bf16[16,1,128]{2,1,0:T(2,128)(2,1)S(1)} async-done(((bf16[16,1,128]{2,1,0:T(2,128)(2,1)}), bf16[16,1,128]{2,1,0:T(2,128)(2,1)S(1)}, u32[]{:S(2)}, u32[]{:S(2)}) %all-to-all-start.9) | async-done | bytes 4128 | tf_op jit(solution)/shard_map/all_to_all | solution.py:29
  192.4 3.9 %all-to-all-start.4 = ((f32[32,256,16]{1,2,0:T(8,128)}), f32[32,256,16]{1,2,0:T(8,128)S(1)}, u32[]{:S(2)}, u32[]{:S(2)}) async-start(f32[32,256,16]{1,2,0:T(8,128)} %broadcast_in_dim.11), calls=%async_computation.4 | async-start | bytes 1048576 | tf_op jit(solution)/shard_map/all_to_all | solution.py:12
  197.1 19.3 %all-to-all-done.4 = f32[32,256,16]{1,2,0:T(8,128)S(1)} async-done(((f32[32,256,16]{1,2,0:T(8,128)}), f32[32,256,16]{1,2,0:T(8,128)S(1)}, u32[]{:S(2)}, u32[]{:S(2)}) %all-to-all-start.4) | async-done | bytes 524320 | tf_op jit(solution)/shard_map/all_to_all | solution.py:12
  217.1 4.5 %all-to-all-start.10 = ((bf16[16,1,128]{2,1,0:T(2,128)(2,1)}), bf16[16,1,128]{2,1,0:T(2,128)(2,1)S(1)}, u32[]{:S(2)}, u32[]{:S(2)}) async-start(bf16[16,1,128]{2,1,0:T(2,128)(2,1)} %broadcast_in_dim.14), calls=%async_computation.10 | async-start | bytes 16384 | tf_op jit(solution)/shard_map/all_to_all | solution.py:12
  221.6 7.1 %all-to-all-done.10 = bf16[16,1,128]{2,1,0:T(2,128)(2,1)S(1)} async-done(((bf16[16,1,128]{2,1,0:T(2,128)(2,1)}), bf16[16,1,128]{2,1,0:T(2,128)(2,1)S(1)}, u32[]{:S(2)}, u32[]{:S(2)}) %all-to-all-start.10) | async-done | bytes 4128 | tf_op jit(solution)/shard_map/all_to_all | solution.py:12
  228.7 4.7 %all-to-all-start.7 = ((bf16[16,16,128]{2,1,0:T(8,128)(2,1)}), bf16[16,16,128]{2,1,0:T(8,128)(2,1)S(1)}, u32[]{:S(2)}, u32[]{:S(2)}) async-start(bf16[16,16,128]{2,1,0:T(8,128)(2,1)} %convolution_convert_fusion.2), calls=%async_computation.7 | async-start | bytes 131072 | tf_op jit(solution)/shard_map/all_to_all | solution.py:29
  234.5 6.6 %all-to-all-done.7 = bf16[16,16,128]{2,1,0:T(8,128)(2,1)S(1)} async-done(((bf16[16,16,128]{2,1,0:T(8,128)(2,1)}), bf16[16,16,128]{2,1,0:T(8,128)(2,1)S(1)}, u32[]{:S(2)}, u32[]{:S(2)}) %all-to-all-start.7) | async-done | bytes 65568 | tf_op jit(solution)/shard_map/all_to_all | solution.py:29
  241.1 4.4 %all-to-all-start.5 = ((bf16[16,448,16]{1,2,0:T(8,128)(2,1)}), bf16[16,448,16]{1,2,0:T(8,128)(2,1)S(1)}, u32[]{:S(2)}, u32[]{:S(2)}) async-start(bf16[16,448,16]{1,2,0:T(8,128)(2,1)} %bitcast.20), calls=%async_computation.5 | async-start | bytes 524288 | tf_op jit(solution)/shard_map/all_to_all | solution.py:29
  245.5 9.1 %all-to-all-done.5 = bf16[16,448,16]{1,2,0:T(8,128)(2,1)S(1)} async-done(((bf16[16,448,16]{1,2,0:T(8,128)(2,1)}), bf16[16,448,16]{1,2,0:T(8,128)(2,1)S(1)}, u32[]{:S(2)}, u32[]{:S(2)}) %all-to-all-start.5) | async-done | bytes 229408 | tf_op jit(solution)/shard_map/all_to_all | solution.py:29
  255.2 4.2 %all-to-all-start.8 = ((bf16[16,16,128]{2,1,0:T(8,128)(2,1)}), bf16[16,16,128]{2,1,0:T(8,128)(2,1)S(1)}, u32[]{:S(2)}, u32[]{:S(2)}) async-start(bf16[16,16,128]{2,1,0:T(8,128)(2,1)} %broadcast_in_dim.13), calls=%async_computation.8 | async-start | bytes 131072 | tf_op jit(solution)/shard_map/all_to_all | solution.py:12
  259.4 7.6 %all-to-all-done.8 = bf16[16,16,128]{2,1,0:T(8,128)(2,1)S(1)} async-done(((bf16[16,16,128]{2,1,0:T(8,128)(2,1)}), bf16[16,16,128]{2,1,0:T(8,128)(2,1)S(1)}, u32[]{:S(2)}, u32[]{:S(2)}) %all-to-all-start.8) | async-done | bytes 65568 | tf_op jit(solution)/shard_map/all_to_all | solution.py:12
  267.7 4.3 %all-to-all-start.6 = ((bf16[16,448,16]{1,2,0:T(8,128)(2,1)}), bf16[16,448,16]{1,2,0:T(8,128)(2,1)S(1)}, u32[]{:S(2)}, u32[]{:S(2)}) async-start(bf16[16,448,16]{1,2,0:T(8,128)(2,1)} %broadcast_in_dim.12), calls=%async_computation.6 | async-start | bytes 524288 | tf_op jit(solution)/shard_map/all_to_all | solution.py:12
  273.4 7.8 %all-to-all-done.6 = bf16[16,448,16]{1,2,0:T(8,128)(2,1)S(1)} async-done(((bf16[16,448,16]{1,2,0:T(8,128)(2,1)}), bf16[16,448,16]{1,2,0:T(8,128)(2,1)S(1)}, u32[]{:S(2)}, u32[]{:S(2)}) %all-to-all-start.6) | async-done | bytes 229408 | tf_op jit(solution)/shard_map/all_to_all | solution.py:12
  281.2 3.8 %fusion.45 = f32[256,448]{0,1:T(8,128)S(1)} fusion(bf16[256,4096]{1,0:T(8,128)(2,1)} %all-gather.2.cloned.1.call-done, bf16[448,4096]{1,0:T(8,128)(2,1)} %param.8), kind=kOutput, calls=%fused_computation.67 | convolution fusion | flops 939524096 | bytes 6225920 | tf_op jit(solution)/shard_map/dot_general | solution.py:129
  (56 shorter events, 12.2 us)
Async XLA Ops:
  7.2 1.7 copy-start
  7.2 35.8 %copy-start.6 = (bf16[16,16,128]{2,1,0:T(8,128)(2,1)S(1)}, bf16[16,16,128]{2,1,0:T(8,128)(2,1)}, u32[]{:S(2)}) copy-start(bf16[16,16,128]{2,1,0:T(8,128)(2,1)} %param.10) | copy-start | bytes 196612
  44.8 4.2 %copy-start.3 = (bf16[256,448]{0,1:T(8,128)(2,1)S(1)}, bf16[256,448]{0,1:T(8,128)(2,1)}, u32[]{:S(2)}) copy-start(bf16[256,448]{0,1:T(8,128)(2,1)} %param.7) | copy-start | bytes 688132
  44.8 56.0 %all-to-all-start.2 = ((bf16[32,16,16,128]{3,2,1,0:T(8,128)(2,1)}), bf16[32,16,16,128]{3,2,1,0:T(8,128)(2,1)S(1)}, u32[]{:S(2)}, u32[]{:S(2)}) async-start(bf16[32,16,16,128]{3,2,1,0:T(8,128)(2,1)} %stack.2), calls=%async_computation.2 | async-start | bytes 4194304 | tf_op jit(solution)/shard_map/all_to_all | solution.py:86
  100.8 1.3 copy-start.1
  102.1 56.4 %all-to-all-start = ((bf16[32,256,128]{2,1,0:T(8,128)(2,1)}), bf16[32,256,128]{2,1,0:T(8,128)(2,1)S(1)}, u32[]{:S(2)}, u32[]{:S(2)}) async-start(bf16[32,256,128]{2,1,0:T(8,128)(2,1)} %bitcast.101), calls=%async_computation | async-start | bytes 4194304 | tf_op jit(solution)/shard_map/all_to_all | solution.py:29
  109.7 4.5 %copy-start.2 = (bf16[32,16,16,128]{3,2,1,0:T(8,128)(2,1)S(1)}, bf16[32,16,16,128]{3,2,1,0:T(8,128)(2,1)}, u32[]{:S(2)}) copy-start(bf16[32,16,16,128]{3,2,1,0:T(8,128)(2,1)} %copy-done.1) | copy-start | bytes 6291460
  116.9 58.0 %copy-start.4 = (bf16[256,128]{1,0:T(8,128)(2,1)S(1)}, bf16[256,128]{1,0:T(8,128)(2,1)}, u32[]{:S(2)}) copy-start(bf16[256,128]{1,0:T(8,128)(2,1)} %param.13) | copy-start | bytes 196612
  117.0 58.0 %copy-start.7 = (bf16[16,128]{1,0:T(8,128)(2,1)S(1)}, bf16[16,128]{1,0:T(8,128)(2,1)}, u32[]{:S(2)}) copy-start(bf16[16,128]{1,0:T(8,128)(2,1)} %param.11) | copy-start | bytes 12292
  158.5 16.5 %all-to-all-start.3 = ((bf16[32,16,128]{2,1,0:T(8,128)(2,1)}), bf16[32,16,128]{2,1,0:T(8,128)(2,1)S(1)}, u32[]{:S(2)}, u32[]{:S(2)}) async-start(bf16[32,16,128]{2,1,0:T(8,128)(2,1)} %copy.23), calls=%async_computation.3 | async-start | bytes 262144 | tf_op jit(solution)/shard_map/all_to_all | solution.py:29
  163.0 118.2 %all-gather.2.cloned.1.call-start = ((), (), s32[]{:S(2)}) async-start(), calls=%async_computation.11 | async-start | bytes 2162688 | tf_op jit(solution)/shard_map/all_gather | solution.py:130
  176.0 20.3 %copy-start.5 = (bf16[256,128]{1,0:T(8,128)(2,1)S(1)}, bf16[256,128]{1,0:T(8,128)(2,1)}, u32[]{:S(2)}) copy-start(bf16[256,128]{1,0:T(8,128)(2,1)} %get-tuple-element.5) | copy-start | bytes 196612
  176.9 14.7 %all-to-all-start.9 = ((bf16[16,1,128]{2,1,0:T(2,128)(2,1)}), bf16[16,1,128]{2,1,0:T(2,128)(2,1)S(1)}, u32[]{:S(2)}, u32[]{:S(2)}) async-start(bf16[16,1,128]{2,1,0:T(2,128)(2,1)} %copy.25), calls=%async_computation.9 | async-start | bytes 16384 | tf_op jit(solution)/shard_map/all_to_all | solution.py:29
  192.4 24.1 %all-to-all-start.4 = ((f32[32,256,16]{1,2,0:T(8,128)}), f32[32,256,16]{1,2,0:T(8,128)S(1)}, u32[]{:S(2)}, u32[]{:S(2)}) async-start(f32[32,256,16]{1,2,0:T(8,128)} %broadcast_in_dim.11), calls=%async_computation.4 | async-start | bytes 1048576 | tf_op jit(solution)/shard_map/all_to_all | solution.py:12
  217.1 11.6 %all-to-all-start.10 = ((bf16[16,1,128]{2,1,0:T(2,128)(2,1)}), bf16[16,1,128]{2,1,0:T(2,128)(2,1)S(1)}, u32[]{:S(2)}, u32[]{:S(2)}) async-start(bf16[16,1,128]{2,1,0:T(2,128)(2,1)} %broadcast_in_dim.14), calls=%async_computation.10 | async-start | bytes 16384 | tf_op jit(solution)/shard_map/all_to_all | solution.py:12
  228.7 12.4 %all-to-all-start.7 = ((bf16[16,16,128]{2,1,0:T(8,128)(2,1)}), bf16[16,16,128]{2,1,0:T(8,128)(2,1)S(1)}, u32[]{:S(2)}, u32[]{:S(2)}) async-start(bf16[16,16,128]{2,1,0:T(8,128)(2,1)} %convolution_convert_fusion.2), calls=%async_computation.7 | async-start | bytes 131072 | tf_op jit(solution)/shard_map/all_to_all | solution.py:29
  241.1 13.5 %all-to-all-start.5 = ((bf16[16,448,16]{1,2,0:T(8,128)(2,1)}), bf16[16,448,16]{1,2,0:T(8,128)(2,1)S(1)}, u32[]{:S(2)}, u32[]{:S(2)}) async-start(bf16[16,448,16]{1,2,0:T(8,128)(2,1)} %bitcast.20), calls=%async_computation.5 | async-start | bytes 524288 | tf_op jit(solution)/shard_map/all_to_all | solution.py:29
  255.2 11.8 %all-to-all-start.8 = ((bf16[16,16,128]{2,1,0:T(8,128)(2,1)}), bf16[16,16,128]{2,1,0:T(8,128)(2,1)S(1)}, u32[]{:S(2)}, u32[]{:S(2)}) async-start(bf16[16,16,128]{2,1,0:T(8,128)(2,1)} %broadcast_in_dim.13), calls=%async_computation.8 | async-start | bytes 131072 | tf_op jit(solution)/shard_map/all_to_all | solution.py:12
  267.7 13.5 %all-to-all-start.6 = ((bf16[16,448,16]{1,2,0:T(8,128)(2,1)}), bf16[16,448,16]{1,2,0:T(8,128)(2,1)S(1)}, u32[]{:S(2)}, u32[]{:S(2)}) async-start(bf16[16,448,16]{1,2,0:T(8,128)(2,1)} %broadcast_in_dim.12), calls=%async_computation.6 | async-start | bytes 524288 | tf_op jit(solution)/shard_map/all_to_all | solution.py:12
Sparse Core Ops, SparseCore 0:
  176.2 80.3 all-gather.1
